TPU v7x, 256 devices: a whole 4x4x8 slice. The times are simulated.
256 devices in a mesh: dp: 32 (over x, y, core), etp: 8 (over z).
Axes of the slice: x: 4, y: 4, z: 8, core: 2. Of those that a mesh axis runs over, the one named last changes fastest.
Arguments:
- tokens: bfloat16 [8192, 3072], P('dp'), may hold values from -6 to 6
- cotangent: bfloat16 [8192, 3072], P('dp'), may hold values from -6 to 6
- w_gate: float32 [2, 3072, 6144], P(None, 'dp', 'etp'), may hold values from -0.109375 to 0.109375
- w_up: float32 [2, 3072, 6144], P(None, 'dp', 'etp'), may hold values from -0.109375 to 0.109375
- w_down: float32 [2, 6144, 3072], P(None, 'etp', 'dp'), may hold values from -0.078125 to 0.078125
- slot_token: int32 [16384], P('dp'), may hold values from 0 to 255, as said below
- slot_gate: int32 [16384], P('dp'), may hold values from 0 to 16
- block_expert: int32 [128], P('dp'), may hold values from 0 to 2, as said below
Outputs:
- combined: bfloat16 [8192, 3072], P('dp', 'etp')
- input_grad: bfloat16 [8192, 3072], P('dp', 'etp')
Inputs may be any that keep to these rules, and one draw needn't show every extreme that they name: `slot_token`: within the live blocks of one expert on one dp index no token repeats, so each expert has at most 2 live blocks there. `block_expert`: blocks of the experts and padding blocks stand in any order; each expert has at most 2 blocks on one dp index, and on some dp index every block is live.
All inputs are finite; a program needn't handle non-finite values.
Results may differ from a plain program's by a relative error of at most 0.014.
Values may be sent and summed in bfloat16 or wider, within the bound.
A program may use at most 128 MiB of HBM per device.

v0:
```python
import jax
import jax.numpy as jnp
from jax import lax
from jax.sharding import PartitionSpec as P

gate_steps = 16.0


def block_terms(
    gate_mat,
    up_mat,
    down_mat,
    tokens,
    cotangent,
    slot_token,
    scale,
    block_index,
    block_rows,
    totals,
):
    y_total, dx_total = totals
    row_start = block_index * block_rows
    token_rows = lax.dynamic_slice_in_dim(slot_token, row_start, block_rows, 0)
    gate_scale = lax.dynamic_slice_in_dim(scale, row_start, block_rows, 0)[:, None]
    inputs = tokens[token_rows]
    upstream = cotangent[token_rows]
    gate_pre = jnp.dot(inputs, gate_mat, preferred_element_type=jnp.float32)
    up_pre = jnp.dot(inputs, up_mat, preferred_element_type=jnp.float32)
    squash = jax.nn.sigmoid(gate_pre)
    active = gate_pre * squash
    hidden = (active * up_pre).astype(jnp.bfloat16)
    produced = jnp.dot(hidden, down_mat, preferred_element_type=jnp.float32) * gate_scale
    d_out = (gate_scale * upstream.astype(jnp.float32)).astype(jnp.bfloat16)
    contract_last = (((1,), (1,)), ((), ()))
    d_hidden = lax.dot_general(d_out, down_mat, contract_last, preferred_element_type=jnp.float32)
    d_pre = (d_hidden * up_pre * squash * (1.0 + gate_pre * (1.0 - squash))).astype(jnp.bfloat16)
    d_up = (d_hidden * active).astype(jnp.bfloat16)
    backward = lax.dot_general(d_pre, gate_mat, contract_last, preferred_element_type=jnp.float32)
    backward = backward + lax.dot_general(
        d_up, up_mat, contract_last, preferred_element_type=jnp.float32
    )
    return (y_total.at[token_rows].add(produced), dx_total.at[token_rows].add(backward))


def shards(tokens, cotangent, w_gate, w_up, w_down, slot_token, slot_gate, block_expert):
    experts_count = w_gate.shape[0]
    block_count = block_expert.shape[0]
    block_rows = slot_token.shape[0] // block_count
    scale = slot_gate.astype(jnp.float32) / gate_steps
    gate_low = w_gate.astype(jnp.bfloat16)
    up_low = w_up.astype(jnp.bfloat16)
    down_low = w_down.astype(jnp.bfloat16)
    zeroed = jnp.zeros(tokens.shape, jnp.float32)
    totals = (zeroed, zeroed)

    def skip_block(state):
        return state

    gate_all, up_all = (
        lax.all_gather(gate_low, "dp", axis=1, tiled=True),
        lax.all_gather(up_low, "dp", axis=1, tiled=True),
    )
    down_all = lax.all_gather(down_low, "dp", axis=2, tiled=True)

    def visit_all(block_index, state):
        expert = block_expert[block_index]
        chosen = jnp.minimum(expert, experts_count - 1)

        def compute_block(inner):
            gate_mat = lax.dynamic_index_in_dim(gate_all, chosen, 0, keepdims=False)
            up_mat = lax.dynamic_index_in_dim(up_all, chosen, 0, keepdims=False)
            down_mat = lax.dynamic_index_in_dim(down_all, chosen, 0, keepdims=False)
            return block_terms(
                gate_mat,
                up_mat,
                down_mat,
                tokens,
                cotangent,
                slot_token,
                scale,
                block_index,
                block_rows,
                inner,
            )

        return lax.cond(expert < experts_count, compute_block, skip_block, state)

    totals = lax.fori_loop(0, block_count, visit_all, totals)
    combined, input_grad = (
        lax.psum_scatter(
            totals[0].astype(jnp.bfloat16), "etp", scatter_dimension=1, tiled=True
        ).astype(jnp.float32),
        lax.psum_scatter(
            totals[1].astype(jnp.bfloat16), "etp", scatter_dimension=1, tiled=True
        ).astype(jnp.float32),
    )
    return (combined.astype(jnp.bfloat16), input_grad.astype(jnp.bfloat16))


def solution(mesh):
    in_specs = (
        P("dp", None),
        P("dp", None),
        P(None, "dp", "etp"),
        P(None, "dp", "etp"),
        P(None, "etp", "dp"),
        P("dp"),
        P("dp"),
        P("dp"),
    )
    out_specs = (P("dp", "etp"), P("dp", "etp"))
    return jax.shard_map(shards, mesh=mesh, in_specs=in_specs, out_specs=out_specs, check_vma=False)
```

profile of v0, /device:TPU:2, one launch (start us, length us, event | category | flops | bytes accessed | tf_op | source)
XLA Modules:
  0.0 489.7 jit_solution(1903295765239692804)
XLA Ops:
  7.2 2.2 copy.18
  9.5 1.8 convert_element_type.44
  11.4 1.8 convert_element_type.45
  13.3 60.4 %all-gather.8.cloned.1.call-done = bf16[2,768,3072]{1,0,2:T(2,128)(2,1)} async-done(((bf16[2,768,96]{1,0,2:T(2,128)(2,1)}), bf16[2,768,3072]{1,0,2:T(2,128)(2,1)}) %all-gather.8.cloned.1.call-update) | async-done | bytes 9437200 | tf_op jit(solution)/shard_map/all_gather | solution.py:63
  73.7 23.8 %copy.12 = bf16[2,768,3072]{2,1,0:T(8,128)(2,1)} copy(bf16[2,768,3072]{1,0,2:T(2,128)(2,1)} %all-gather.8.cloned.1.call-done) | data formatting | bytes 18874368 | tf_op jit(solution)/shard_map/while | solution.py:88
  97.5 38.7 %all-gather.4.cloned.1.call-done = bf16[2,3072,768]{2,1,0:T(8,128)(2,1)} async-done(((bf16[2,96,768]{2,1,0:T(8,128)(2,1)}), bf16[2,3072,768]{2,1,0:T(8,128)(2,1)}) %all-gather.4.cloned.1.call-update) | async-done | bytes 9437200 | tf_op jit(solution)/shard_map/all_gather | solution.py:60
  136.2 62.5 %all-gather.6.cloned.1.call-done = bf16[2,3072,768]{2,1,0:T(8,128)(2,1)} async-done(((bf16[2,96,768]{2,1,0:T(8,128)(2,1)}), bf16[2,3072,768]{2,1,0:T(8,128)(2,1)}) %all-gather.6.cloned.1.call-update) | async-done | bytes 9437200 | tf_op jit(solution)/shard_map/all_gather | solution.py:61
  199.0 2.1 broadcast_in_dim.4.clone
  201.1 194.1 %while.15 = (s32[]{:T(128)}, f32[256,3072]{1,0:T(8,128)S(1)}, f32[256,3072]{1,0:T(8,128)}, s32[4]{0:T(128)S(1)}, s32[512]{0:T(512)}, /*index=5*/bf16[256,3072]{1...) while((s32[]{:T(128)}, f32[256,3072]{1,0:T(8,128)S(1)}, ...), condition=%wide.region_5.6_spmd, body=%wide.region_0.5_spmd.sunk | while | flops 3628795392 | bytes 59779048 | solution.py:88
  202.4 47.3 %conditional.2 = ((f32[256,3072]{1,0:T(8,128)S(1)}, f32[256,3072]{1,0:T(8,128)})) conditional(s32[]{:T(128)} %convert_element_type.63, (f32[256,3072]{1,0:T(8,128)S(1)}, f32[256,3072]{1,0:T(8,128)}) %tuple.42, (s32[]{:T(128)}, s32[512]{0:T(512)}, bf16[256,3072]{1,0:T(8,128)(2,1)}, s32[]{:T(128)}, bf16[2,3072,768]{2,1,0:T(8,128)(2,1)}, ...), branch_computations={%region_1.0_spmd, %region_2.4_spmd} | conditional | flops 3628795392 | bytes 59778792 | solution.py:86
  203.0 0.8 compare_select_fusion
  203.8 4.3 gather_fusion.1
  208.2 5.0 %fusion = f32[128,768]{1,0:T(8,128)} fusion(bf16[2,768,3072]{2,1,0:T(8,128)(2,1)} %get-tuple-element.210, s32[]{:T(128)S(6)} %select_n.21, bf16[128,3072]{1,0:T(8,128)(2,1)} %gather_fusion.1, f32[128]{0:T(128)S(1)} %dynamic_slice.22), kind=kOutput, calls=%fused_computation.4 | convolution fusion | flops 605159424 | bytes 5898756 | tf_op jit(solution)/shard_map/while/body/eval_jaxpr/cond/branch_1_fun/dot_general | solution.py:35
  213.3 4.3 gather_fusion
  217.6 3.4 fusion.10
  221.0 4.1 fusion.4
  225.1 3.1 fusion.6
  228.2 5.3 %fusion.18 = f32[128,3072]{1,0:T(8,128)} fusion(f32[128,3072]{1,0:T(8,128)S(1)} %fusion.4, bf16[2,3072,768]{2,1,0:T(8,128)(2,1)} %get-tuple-element.207, s32[]{:T(128)S(6)} %select_n.21, f32[128,768]{1,0:T(8,128)S(1)} %fusion.10, f32[128,768]{1,0:T(8,128)S(1)} %copy-done.2, f32[128,768]{1,0:T(8,128)S(1)} %fusion.6), kind=kOutput, calls=%fused_computation.22 | convolution fusion | flops 605356032 | bytes 9043972 | tf_op jit(solution)/shard_map/while/body/eval_jaxpr/cond/branch_1_fun/dot_general | solution.py:38
  233.5 7.0 %scatter_fusion.1 = f32[256,3072]{1,0:T(8,128)} fusion(f32[256,3072]{1,0:T(8,128)} %get-tuple-element.212, s32[128]{0:T(128)S(1)} %compare_select_fusion, f32[128,3072]{1,0:T(8,128)} %fusion.18), kind=kCustom, calls=%fused_computation.3 | custom fusion | flops 393216 | bytes 4719104 | tf_op jit(solution)/shard_map/while/body/eval_jaxpr/cond/branch_1_fun/scatter-add | solution.py:42
  240.6 4.4 fusion.21
  245.0 4.6 scatter_fusion
  250.9 47.3 %conditional.2 = ((f32[256,3072]{1,0:T(8,128)S(1)}, f32[256,3072]{1,0:T(8,128)})) conditional(s32[]{:T(128)} %convert_element_type.63, (f32[256,3072]{1,0:T(8,128)S(1)}, f32[256,3072]{1,0:T(8,128)}) %tuple.42, (s32[]{:T(128)}, s32[512]{0:T(512)}, bf16[256,3072]{1,0:T(8,128)(2,1)}, s32[]{:T(128)}, bf16[2,3072,768]{2,1,0:T(8,128)(2,1)}, ...), branch_computations={%region_1.0_spmd, %region_2.4_spmd} | conditional | flops 3628795392 | bytes 59778792 | solution.py:86
  251.6 0.8 compare_select_fusion
  252.4 4.3 gather_fusion.1
  256.8 5.0 %fusion = f32[128,768]{1,0:T(8,128)} fusion(bf16[2,768,3072]{2,1,0:T(8,128)(2,1)} %get-tuple-element.210, s32[]{:T(128)S(6)} %select_n.21, bf16[128,3072]{1,0:T(8,128)(2,1)} %gather_fusion.1, f32[128]{0:T(128)S(1)} %dynamic_slice.22), kind=kOutput, calls=%fused_computation.4 | convolution fusion | flops 605159424 | bytes 5898756 | tf_op jit(solution)/shard_map/while/body/eval_jaxpr/cond/branch_1_fun/dot_general | solution.py:35
  261.8 4.3 gather_fusion
  266.2 3.4 fusion.10
  269.6 4.0 fusion.4
  273.6 3.1 fusion.6
  276.8 5.3 %fusion.18 = f32[128,3072]{1,0:T(8,128)} fusion(f32[128,3072]{1,0:T(8,128)S(1)} %fusion.4, bf16[2,3072,768]{2,1,0:T(8,128)(2,1)} %get-tuple-element.207, s32[]{:T(128)S(6)} %select_n.21, f32[128,768]{1,0:T(8,128)S(1)} %fusion.10, f32[128,768]{1,0:T(8,128)S(1)} %copy-done.2, f32[128,768]{1,0:T(8,128)S(1)} %fusion.6), kind=kOutput, calls=%fused_computation.22 | convolution fusion | flops 605356032 | bytes 9043972 | tf_op jit(solution)/shard_map/while/body/eval_jaxpr/cond/branch_1_fun/dot_general | solution.py:38
  282.1 7.0 %scatter_fusion.1 = f32[256,3072]{1,0:T(8,128)} fusion(f32[256,3072]{1,0:T(8,128)} %get-tuple-element.212, s32[128]{0:T(128)S(1)} %compare_select_fusion, f32[128,3072]{1,0:T(8,128)} %fusion.18), kind=kCustom, calls=%fused_computation.3 | custom fusion | flops 393216 | bytes 4719104 | tf_op jit(solution)/shard_map/while/body/eval_jaxpr/cond/branch_1_fun/scatter-add | solution.py:42
  289.1 4.4 fusion.21
  293.6 4.6 scatter_fusion
  299.5 47.3 %conditional.2 = ((f32[256,3072]{1,0:T(8,128)S(1)}, f32[256,3072]{1,0:T(8,128)})) conditional(s32[]{:T(128)} %convert_element_type.63, (f32[256,3072]{1,0:T(8,128)S(1)}, f32[256,3072]{1,0:T(8,128)}) %tuple.42, (s32[]{:T(128)}, s32[512]{0:T(512)}, bf16[256,3072]{1,0:T(8,128)(2,1)}, s32[]{:T(128)}, bf16[2,3072,768]{2,1,0:T(8,128)(2,1)}, ...), branch_computations={%region_1.0_spmd, %region_2.4_spmd} | conditional | flops 3628795392 | bytes 59778792 | solution.py:86
  300.1 0.8 compare_select_fusion
  300.9 4.3 gather_fusion.1
  305.3 5.0 %fusion = f32[128,768]{1,0:T(8,128)} fusion(bf16[2,768,3072]{2,1,0:T(8,128)(2,1)} %get-tuple-element.210, s32[]{:T(128)S(6)} %select_n.21, bf16[128,3072]{1,0:T(8,128)(2,1)} %gather_fusion.1, f32[128]{0:T(128)S(1)} %dynamic_slice.22), kind=kOutput, calls=%fused_computation.4 | convolution fusion | flops 605159424 | bytes 5898756 | tf_op jit(solution)/shard_map/while/body/eval_jaxpr/cond/branch_1_fun/dot_general | solution.py:35
  310.3 4.3 gather_fusion
  314.7 3.4 fusion.10
  318.1 4.0 fusion.4
  322.2 3.1 fusion.6
  325.3 5.3 %fusion.18 = f32[128,3072]{1,0:T(8,128)} fusion(f32[128,3072]{1,0:T(8,128)S(1)} %fusion.4, bf16[2,3072,768]{2,1,0:T(8,128)(2,1)} %get-tuple-element.207, s32[]{:T(128)S(6)} %select_n.21, f32[128,768]{1,0:T(8,128)S(1)} %fusion.10, f32[128,768]{1,0:T(8,128)S(1)} %copy-done.2, f32[128,768]{1,0:T(8,128)S(1)} %fusion.6), kind=kOutput, calls=%fused_computation.22 | convolution fusion | flops 605356032 | bytes 9043972 | tf_op jit(solution)/shard_map/while/body/eval_jaxpr/cond/branch_1_fun/dot_general | solution.py:38
  330.6 7.0 %scatter_fusion.1 = f32[256,3072]{1,0:T(8,128)} fusion(f32[256,3072]{1,0:T(8,128)} %get-tuple-element.212, s32[128]{0:T(128)S(1)} %compare_select_fusion, f32[128,3072]{1,0:T(8,128)} %fusion.18), kind=kCustom, calls=%fused_computation.3 | custom fusion | flops 393216 | bytes 4719104 | tf_op jit(solution)/shard_map/while/body/eval_jaxpr/cond/branch_1_fun/scatter-add | solution.py:42
  337.6 4.4 fusion.21
  342.1 4.6 scatter_fusion
  348.0 47.3 %conditional.2 = ((f32[256,3072]{1,0:T(8,128)S(1)}, f32[256,3072]{1,0:T(8,128)})) conditional(s32[]{:T(128)} %convert_element_type.63, (f32[256,3072]{1,0:T(8,128)S(1)}, f32[256,3072]{1,0:T(8,128)}) %tuple.42, (s32[]{:T(128)}, s32[512]{0:T(512)}, bf16[256,3072]{1,0:T(8,128)(2,1)}, s32[]{:T(128)}, bf16[2,3072,768]{2,1,0:T(8,128)(2,1)}, ...), branch_computations={%region_1.0_spmd, %region_2.4_spmd} | conditional | flops 3628795392 | bytes 59778792 | solution.py:86
  349.4 4.3 gather_fusion.1
  353.8 5.0 %fusion = f32[128,768]{1,0:T(8,128)} fusion(bf16[2,768,3072]{2,1,0:T(8,128)(2,1)} %get-tuple-element.210, s32[]{:T(128)S(6)} %select_n.21, bf16[128,3072]{1,0:T(8,128)(2,1)} %gather_fusion.1, f32[128]{0:T(128)S(1)} %dynamic_slice.22), kind=kOutput, calls=%fused_computation.4 | convolution fusion | flops 605159424 | bytes 5898756 | tf_op jit(solution)/shard_map/while/body/eval_jaxpr/cond/branch_1_fun/dot_general | solution.py:35
  358.9 4.3 gather_fusion
  363.2 3.4 fusion.10
  366.6 4.0 fusion.4
  370.7 3.1 fusion.6
  373.8 5.3 %fusion.18 = f32[128,3072]{1,0:T(8,128)} fusion(f32[128,3072]{1,0:T(8,128)S(1)} %fusion.4, bf16[2,3072,768]{2,1,0:T(8,128)(2,1)} %get-tuple-element.207, s32[]{:T(128)S(6)} %select_n.21, f32[128,768]{1,0:T(8,128)S(1)} %fusion.10, f32[128,768]{1,0:T(8,128)S(1)} %copy-done.2, f32[128,768]{1,0:T(8,128)S(1)} %fusion.6), kind=kOutput, calls=%fused_computation.22 | convolution fusion | flops 605356032 | bytes 9043972 | tf_op jit(solution)/shard_map/while/body/eval_jaxpr/cond/branch_1_fun/dot_general | solution.py:38
  379.1 7.0 %scatter_fusion.1 = f32[256,3072]{1,0:T(8,128)} fusion(f32[256,3072]{1,0:T(8,128)} %get-tuple-element.212, s32[128]{0:T(128)S(1)} %compare_select_fusion, f32[128,3072]{1,0:T(8,128)} %fusion.18), kind=kCustom, calls=%fused_computation.3 | custom fusion | flops 393216 | bytes 4719104 | tf_op jit(solution)/shard_map/while/body/eval_jaxpr/cond/branch_1_fun/scatter-add | solution.py:42
  386.2 4.4 fusion.21
  390.6 4.6 scatter_fusion
  395.3 1.4 convert_element_type.48
  396.6 2.8 copy.13
  399.5 1.4 convert_element_type.49
  400.9 2.6 copy.15
  403.5 36.2 %reduce-scatter.7.cloned.1.call-done = bf16[384,256]{1,0:T(8,128)(2,1)} async-done(((bf16[3072,256]{1,0:T(8,128)(2,1)}), bf16[384,256]{1,0:T(8,128)(2,1)}) %reduce-scatter.7.cloned.1.call-update) | async-done | bytes 196624
  439.7 1.7 copy.14
  441.4 40.0 %reduce-scatter.9.cloned.1.call-done = bf16[384,256]{1,0:T(8,128)(2,1)} async-done(((bf16[3072,256]{1,0:T(8,128)(2,1)}), bf16[384,256]{1,0:T(8,128)(2,1)}) %reduce-scatter.9.cloned.1.call-update) | async-done | bytes 196624
  481.4 1.7 copy.16
  (55 shorter events, 4.1 us)
Async XLA Ops:
  7.2 6.1 %copy-start.4 = (s32[512]{0:T(512)S(1)}, s32[512]{0:T(512)}, u32[]{:S(2)}) copy-start(s32[512]{0:T(512)} %param.18) | copy-start | bytes 6148
  7.2 66.6 %all-gather.8.cloned.1.call-start = ((), (), s32[]{:S(2)}) async-start(), calls=%async_computation.4 | async-start | bytes 9732096 | tf_op jit(solution)/shard_map/all_gather | solution.py:63
  9.5 126.7 %all-gather.4.cloned.1.call-start = ((), (), s32[]{:S(2)}) async-start(), calls=%async_computation.2 | async-start | bytes 9732096 | tf_op jit(solution)/shard_map/all_gather | solution.py:60
  11.4 187.3 %all-gather.6.cloned.1.call-start = ((), (), s32[]{:S(2)}) async-start(), calls=%async_computation.3 | async-start | bytes 9732096 | tf_op jit(solution)/shard_map/all_gather | solution.py:61
  13.2 426.4 %reduce-scatter.7.cloned.1.call-start = ((), (), s32[]{:S(2)}) async-start(), calls=%async_computation.5 | async-start | bytes 1769472
  97.5 103.6 %copy-start.5 = (s32[4]{0:T(128)S(1)}, s32[4]{0:T(128)}, u32[]{:S(2)}) copy-start(s32[4]{0:T(128)} %param.19) | copy-start | bytes 52
  217.6 3.4 copy-start.2
  221.0 4.1 copy-start.1
  228.2 5.3 %copy-start.3 = (f32[128,768]{1,0:T(8,128)}, f32[128,768]{1,0:T(8,128)S(1)}, u32[]{:S(2)}) copy-start(f32[128,768]{1,0:T(8,128)S(1)} %fusion.6) | copy-start | bytes 1179652 | tf_op jit(solution)/shard_map/while/body/eval_jaxpr/cond
  266.1 3.4 copy-start.2
  269.6 4.0 copy-start.1
  276.8 5.3 %copy-start.3 = (f32[128,768]{1,0:T(8,128)}, f32[128,768]{1,0:T(8,128)S(1)}, u32[]{:S(2)}) copy-start(f32[128,768]{1,0:T(8,128)S(1)} %fusion.6) | copy-start | bytes 1179652 | tf_op jit(solution)/shard_map/while/body/eval_jaxpr/cond
  314.7 3.4 copy-start.2
  318.1 4.0 copy-start.1
  325.3 5.3 %copy-start.3 = (f32[128,768]{1,0:T(8,128)}, f32[128,768]{1,0:T(8,128)S(1)}, u32[]{:S(2)}) copy-start(f32[128,768]{1,0:T(8,128)S(1)} %fusion.6) | copy-start | bytes 1179652 | tf_op jit(solution)/shard_map/while/body/eval_jaxpr/cond
  363.2 3.4 copy-start.2
  366.6 4.0 copy-start.1
  373.8 5.3 %copy-start.3 = (f32[128,768]{1,0:T(8,128)}, f32[128,768]{1,0:T(8,128)S(1)}, u32[]{:S(2)}) copy-start(f32[128,768]{1,0:T(8,128)S(1)} %fusion.6) | copy-start | bytes 1179652 | tf_op jit(solution)/shard_map/while/body/eval_jaxpr/cond
  396.6 2.8 copy-start
  399.4 82.0 %reduce-scatter.9.cloned.1.call-start = ((), (), s32[]{:S(2)}) async-start(), calls=%async_computation.6 | async-start | bytes 1769472
Sparse Core Ops, SparseCore 0:
  10.5 63.1 all-gather.7
  76.3 59.8 all-gather.3
  138.8 59.8 all-gather.5
  399.5 40.0 reduce-scatter.6
  442.1 39.2 reduce-scatter.8
where the time goes:
time: 492 us; the launch traced here: 490 us
  waiting for transfers between devices  238 us (48%)
  matrix products  101 us (21%)
  local copies, waits for them, and re-layouts  74.6 us (15%)
  other arithmetic  56.1 us (11%)
  between operations  13.8 us (3%)
  loops' own time  5.68 us (1%)
    unnamed x7, waiting for transfers between devices  76.3 us
    all_gather x1, waiting for transfers between devices, shards(): lax.all_gather(up_low, 'dp', axis=1, tiled=True)  62.5 us
    all_gather x1, waiting for transfers between devices, shards(): down_all = lax.all_gather(down_low, 'dp', axis=2, tiled=True)  60.4 us
    all_gather x1, waiting for transfers between devices, shards(): lax.all_gather(gate_low, 'dp', axis=1, tiled=True)  38.7 us
    scatter-add x4, other arithmetic, block_terms(): dx_total.at[token_rows].add(backward)  28.2 us
    while x1, local copies, waits for them, and re-layouts, shards(): totals = lax.fori_loop(0, block_count, visit_all, totals)  23.8 us
    dot_general x4, matrix products, block_terms(): lax.dot_general(d_pre, gate_mat, contract_last, preferred_element_type=jn...  21.2 us
    dot_general x4, matrix products, block_terms(): lax.dot_general(d_out, down_mat, contract_last, preferred_element_type=jn...  20.1 us
  transfers between devices with their start and end apart: 5, of which 5 were waited for; matrix products, arithmetic and copies ran while one was open for 7% of the time, Pallas kernels for 0%

commit v1 on v0

--- a/solution.py
+++ b/solution.py
@@ -60,7 +60,8 @@
         lax.all_gather(gate_low, "dp", axis=1, tiled=True),
         lax.all_gather(up_low, "dp", axis=1, tiled=True),
     )
-    down_all = lax.all_gather(down_low, "dp", axis=2, tiled=True)
+    repeated = jnp.stack([down_low] * lax.axis_size("dp"))
+    down_all = jnp.concatenate(lax.all_to_all(repeated, "dp", 0, 0), axis=2)
 
     def visit_all(block_index, state):
         expert = block_expert[block_index]

time: 492 us -> 522 us (1.061)
  waiting for transfers between devices: 238 us -> 259 us
  starting transfers between devices: 0.21 us -> 7.97 us
    all_to_all x0 -> x1, waiting for transfers between devices: none -> 136 us  [shards(): down_all = jnp.concatenate(lax.all_to_all(repeated, 'dp', 0, 0), axis=2)]
    all_gather x1 -> x0, waiting for transfers between devices: 60.4 us -> none  [shards(): down_all = lax.all_gather(down_low, 'dp', axis=2, tiled=True)]
    all_gather x1, waiting for transfers between devices: 38.7 us -> 0.01 us  [shards(): lax.all_gather(gate_low, 'dp', axis=1, tiled=True)]
    all_gather x1, waiting for transfers between devices: 62.5 us -> 47.1 us  [shards(): lax.all_gather(up_low, 'dp', axis=1, tiled=True)]
    while x1, local copies, waits for them, and re-layouts: 23.8 us -> 12.7 us  [shards(): totals = lax.fori_loop(0, block_count, visit_all, totals)]
    all_to_all x0 -> x1, local copies, waits for them, and re-layouts: none -> 8.13 us  [shards(): down_all = jnp.concatenate(lax.all_to_all(repeated, 'dp', 0, 0), axis=2)]
    all_to_all x0 -> x1, starting transfers between devices: none -> 7.8 us  [shards(): down_all = jnp.concatenate(lax.all_to_all(repeated, 'dp', 0, 0), axis=2)]
    unnamed x11 -> x10, local copies, waits for them, and re-layouts: 11.1 us -> 8.82 us
  transfers between devices with their start and end apart: 5 -> 5, of which waited for: 5 -> 4; matrix products, arithmetic and copies ran while one was open for 7% -> 7% of each run, Pallas kernels for 0% -> 0%
where the time goes in v1:
time: 522 us; the launch traced here: 520 us
  waiting for transfers between devices  259 us (50%)
  matrix products  101 us (19%)
  local copies, waits for them, and re-layouts  74.3 us (14%)
  other arithmetic  57.2 us (11%)
  between operations  13.8 us (3%)
  starting transfers between devices  7.97 us (2%)
  loops' own time  5.68 us (1%)
    all_to_all x1, waiting for transfers between devices, shards(): down_all = jnp.concatenate(lax.all_to_all(repeated, 'dp', 0, 0), axis=2)  136 us
    unnamed x6, waiting for transfers between devices  76.3 us
    all_gather x1, waiting for transfers between devices, shards(): lax.all_gather(up_low, 'dp', axis=1, tiled=True)  47.1 us
    scatter-add x4, other arithmetic, block_terms(): dx_total.at[token_rows].add(backward)  28.2 us
    dot_general x4, matrix products, block_terms(): lax.dot_general(d_pre, gate_mat, contract_last, preferred_element_type=jn...  21.2 us
    dot_general x4, matrix products, block_terms(): lax.dot_general(d_out, down_mat, contract_last, preferred_element_type=jn...  20.1 us
    scatter-add x4, other arithmetic, block_terms(): y_total.at[token_rows].add(produced)  18.5 us
    dot_general x4, matrix products, block_terms(): jnp.dot(hidden, down_mat, preferred_element_type=jnp.float32) * gate_scale  17.8 us
  transfers between devices with their start and end apart: 5, of which 4 were waited for; matrix products, arithmetic and copies ran while one was open for 7% of the time, Pallas kernels for 0%

profile of v1, /device:TPU:2, one launch (start us, length us, event | category | flops | bytes accessed | tf_op | source)
XLA Modules:
  0.0 519.6 jit_solution(337826109244909726)
XLA Ops:
  7.2 1.8 convert_element_type.44
  9.1 1.8 convert_element_type.45
  10.9 1.1 convert_element_type.46
  12.0 4.8 stack.2
  16.9 7.8 %all-to-all-start = ((bf16[32,2,768,96]{2,3,1,0:T(8,128)(2,1)}), bf16[32,2,768,96]{2,3,1,0:T(8,128)(2,1)}, u32[]{:S(2)}, u32[]{:S(2)}) async-start(bf16[32,2,768,96]{2,3,1,0:T(8,128)(2,1)} %stack.2), calls=%async_computation | async-start | bytes 18874368 | tf_op jit(solution)/shard_map/all_to_all | solution.py:64
  24.7 135.8 %all-to-all-done = bf16[32,2,768,96]{2,3,1,0:T(8,128)(2,1)} async-done(((bf16[32,2,768,96]{2,3,1,0:T(8,128)(2,1)}), bf16[32,2,768,96]{2,3,1,0:T(8,128)(2,1)}, u32[]{:S(2)}, u32[]{:S(2)}) %all-to-all-start) | async-done | bytes 9437216 | tf_op jit(solution)/shard_map/all_to_all | solution.py:64
  160.6 8.1 %copy.12 = bf16[32,2,768,96]{2,3,0,1:T(8,128)(2,1)} copy(bf16[32,2,768,96]{2,3,1,0:T(8,128)(2,1)} %all-to-all-done) | data formatting | bytes 18874368 | tf_op jit(solution)/shard_map/all_to_all | solution.py:64
  168.7 12.7 %copy.13 = bf16[2,768,3072]{2,1,0:T(8,128)(2,1)} copy(bf16[2,768,3072]{1,2,0:T(8,128)(2,1)} %bitcast.31) | data formatting | bytes 18874368 | tf_op jit(solution)/shard_map/while | solution.py:89
  181.4 47.1 %all-gather.5.cloned.1.call-done = bf16[2,3072,768]{2,1,0:T(8,128)(2,1)} async-done(((bf16[2,96,768]{2,1,0:T(8,128)(2,1)}), bf16[2,3072,768]{2,1,0:T(8,128)(2,1)}) %all-gather.5.cloned.1.call-update) | async-done | bytes 9437200 | tf_op jit(solution)/shard_map/all_gather | solution.py:61
  228.9 2.1 broadcast_in_dim.4.clone
  231.0 194.2 %while.15 = (s32[]{:T(128)}, f32[256,3072]{1,0:T(8,128)S(1)}, f32[256,3072]{1,0:T(8,128)}, s32[4]{0:T(128)S(1)}, s32[512]{0:T(512)}, /*index=5*/bf16[256,3072]{1...) while((s32[]{:T(128)}, f32[256,3072]{1,0:T(8,128)S(1)}, ...), condition=%wide.region_5.6_spmd, body=%wide.region_0.5_spmd.sunk | while | flops 3628795392 | bytes 59779048 | solution.py:89
  232.2 47.3 %conditional.2 = ((f32[256,3072]{1,0:T(8,128)S(1)}, f32[256,3072]{1,0:T(8,128)})) conditional(s32[]{:T(128)} %convert_element_type.62, (f32[256,3072]{1,0:T(8,128)S(1)}, f32[256,3072]{1,0:T(8,128)}) %tuple.43, (s32[]{:T(128)}, s32[512]{0:T(512)}, bf16[256,3072]{1,0:T(8,128)(2,1)}, s32[]{:T(128)}, bf16[2,3072,768]{2,1,0:T(8,128)(2,1)}, ...), branch_computations={%region_1.0_spmd, %region_2.4_spmd} | conditional | flops 3628795392 | bytes 59778792 | solution.py:87
  233.7 4.3 gather_fusion.1
  238.1 5.0 fusion
  243.1 4.3 gather_fusion
  247.4 3.4 fusion.10
  250.9 4.0 fusion.4
  254.9 3.1 fusion.6
  258.1 5.3 %fusion.18 = f32[128,3072]{1,0:T(8,128)} fusion(f32[128,3072]{1,0:T(8,128)S(1)} %fusion.4, bf16[2,3072,768]{2,1,0:T(8,128)(2,1)} %get-tuple-element.207, s32[]{:T(128)S(6)} %select_n.21, f32[128,768]{1,0:T(8,128)S(1)} %fusion.10, f32[128,768]{1,0:T(8,128)S(1)} %copy-done.2, f32[128,768]{1,0:T(8,128)S(1)} %fusion.6), kind=kOutput, calls=%fused_computation.22 | convolution fusion | flops 605356032 | bytes 9043972 | tf_op jit(solution)/shard_map/while/body/eval_jaxpr/cond/branch_1_fun/dot_general | solution.py:38
  263.4 7.0 %scatter_fusion.1 = f32[256,3072]{1,0:T(8,128)} fusion(f32[256,3072]{1,0:T(8,128)} %get-tuple-element.212, s32[128]{0:T(128)S(1)} %compare_select_fusion, f32[128,3072]{1,0:T(8,128)} %fusion.18), kind=kCustom, calls=%fused_computation.3 | custom fusion | flops 393216 | bytes 4719104 | tf_op jit(solution)/shard_map/while/body/eval_jaxpr/cond/branch_1_fun/scatter-add | solution.py:42
  270.4 4.4 fusion.21
  274.9 4.6 scatter_fusion
  280.8 47.3 %conditional.2 = ((f32[256,3072]{1,0:T(8,128)S(1)}, f32[256,3072]{1,0:T(8,128)})) conditional(s32[]{:T(128)} %convert_element_type.62, (f32[256,3072]{1,0:T(8,128)S(1)}, f32[256,3072]{1,0:T(8,128)}) %tuple.43, (s32[]{:T(128)}, s32[512]{0:T(512)}, bf16[256,3072]{1,0:T(8,128)(2,1)}, s32[]{:T(128)}, bf16[2,3072,768]{2,1,0:T(8,128)(2,1)}, ...), branch_computations={%region_1.0_spmd, %region_2.4_spmd} | conditional | flops 3628795392 | bytes 59778792 | solution.py:87
  281.5 0.8 compare_select_fusion
  282.2 4.3 gather_fusion.1
  286.6 5.0 fusion
  291.7 4.3 gather_fusion
  296.0 3.4 fusion.10
  299.4 4.0 fusion.4
  303.5 3.1 fusion.6
  306.6 5.3 %fusion.18 = f32[128,3072]{1,0:T(8,128)} fusion(f32[128,3072]{1,0:T(8,128)S(1)} %fusion.4, bf16[2,3072,768]{2,1,0:T(8,128)(2,1)} %get-tuple-element.207, s32[]{:T(128)S(6)} %select_n.21, f32[128,768]{1,0:T(8,128)S(1)} %fusion.10, f32[128,768]{1,0:T(8,128)S(1)} %copy-done.2, f32[128,768]{1,0:T(8,128)S(1)} %fusion.6), kind=kOutput, calls=%fused_computation.22 | convolution fusion | flops 605356032 | bytes 9043972 | tf_op jit(solution)/shard_map/while/body/eval_jaxpr/cond/branch_1_fun/dot_general | solution.py:38
  311.9 7.0 %scatter_fusion.1 = f32[256,3072]{1,0:T(8,128)} fusion(f32[256,3072]{1,0:T(8,128)} %get-tuple-element.212, s32[128]{0:T(128)S(1)} %compare_select_fusion, f32[128,3072]{1,0:T(8,128)} %fusion.18), kind=kCustom, calls=%fused_computation.3 | custom fusion | flops 393216 | bytes 4719104 | tf_op jit(solution)/shard_map/while/body/eval_jaxpr/cond/branch_1_fun/scatter-add | solution.py:42
  319.0 4.4 fusion.21
  323.4 4.6 scatter_fusion
  329.3 47.3 %conditional.2 = ((f32[256,3072]{1,0:T(8,128)S(1)}, f32[256,3072]{1,0:T(8,128)})) conditional(s32[]{:T(128)} %convert_element_type.62, (f32[256,3072]{1,0:T(8,128)S(1)}, f32[256,3072]{1,0:T(8,128)}) %tuple.43, (s32[]{:T(128)}, s32[512]{0:T(512)}, bf16[256,3072]{1,0:T(8,128)(2,1)}, s32[]{:T(128)}, bf16[2,3072,768]{2,1,0:T(8,128)(2,1)}, ...), branch_computations={%region_1.0_spmd, %region_2.4_spmd} | conditional | flops 3628795392 | bytes 59778792 | solution.py:87
  330.8 4.3 gather_fusion.1
  335.2 5.0 fusion
  340.2 4.3 gather_fusion
  344.6 3.4 fusion.10
  348.0 4.0 fusion.4
  352.1 3.1 fusion.6
  355.2 5.3 %fusion.18 = f32[128,3072]{1,0:T(8,128)} fusion(f32[128,3072]{1,0:T(8,128)S(1)} %fusion.4, bf16[2,3072,768]{2,1,0:T(8,128)(2,1)} %get-tuple-element.207, s32[]{:T(128)S(6)} %select_n.21, f32[128,768]{1,0:T(8,128)S(1)} %fusion.10, f32[128,768]{1,0:T(8,128)S(1)} %copy-done.2, f32[128,768]{1,0:T(8,128)S(1)} %fusion.6), kind=kOutput, calls=%fused_computation.22 | convolution fusion | flops 605356032 | bytes 9043972 | tf_op jit(solution)/shard_map/while/body/eval_jaxpr/cond/branch_1_fun/dot_general | solution.py:38
  360.5 7.0 %scatter_fusion.1 = f32[256,3072]{1,0:T(8,128)} fusion(f32[256,3072]{1,0:T(8,128)} %get-tuple-element.212, s32[128]{0:T(128)S(1)} %compare_select_fusion, f32[128,3072]{1,0:T(8,128)} %fusion.18), kind=kCustom, calls=%fused_computation.3 | custom fusion | flops 393216 | bytes 4719104 | tf_op jit(solution)/shard_map/while/body/eval_jaxpr/cond/branch_1_fun/scatter-add | solution.py:42
  367.6 4.4 fusion.21
  372.0 4.6 scatter_fusion
  377.9 47.3 %conditional.2 = ((f32[256,3072]{1,0:T(8,128)S(1)}, f32[256,3072]{1,0:T(8,128)})) conditional(s32[]{:T(128)} %convert_element_type.62, (f32[256,3072]{1,0:T(8,128)S(1)}, f32[256,3072]{1,0:T(8,128)}) %tuple.43, (s32[]{:T(128)}, s32[512]{0:T(512)}, bf16[256,3072]{1,0:T(8,128)(2,1)}, s32[]{:T(128)}, bf16[2,3072,768]{2,1,0:T(8,128)(2,1)}, ...), branch_computations={%region_1.0_spmd, %region_2.4_spmd} | conditional | flops 3628795392 | bytes 59778792 | solution.py:87
  379.4 4.3 gather_fusion.1
  383.8 5.0 fusion
  388.8 4.3 gather_fusion
  393.1 3.4 fusion.10
  396.6 4.0 fusion.4
  400.6 3.1 fusion.6
  403.8 5.3 %fusion.18 = f32[128,3072]{1,0:T(8,128)} fusion(f32[128,3072]{1,0:T(8,128)S(1)} %fusion.4, bf16[2,3072,768]{2,1,0:T(8,128)(2,1)} %get-tuple-element.207, s32[]{:T(128)S(6)} %select_n.21, f32[128,768]{1,0:T(8,128)S(1)} %fusion.10, f32[128,768]{1,0:T(8,128)S(1)} %copy-done.2, f32[128,768]{1,0:T(8,128)S(1)} %fusion.6), kind=kOutput, calls=%fused_computation.22 | convolution fusion | flops 605356032 | bytes 9043972 | tf_op jit(solution)/shard_map/while/body/eval_jaxpr/cond/branch_1_fun/dot_general | solution.py:38
  409.1 7.0 %scatter_fusion.1 = f32[256,3072]{1,0:T(8,128)} fusion(f32[256,3072]{1,0:T(8,128)} %get-tuple-element.212, s32[128]{0:T(128)S(1)} %compare_select_fusion, f32[128,3072]{1,0:T(8,128)} %fusion.18), kind=kCustom, calls=%fused_computation.3 | custom fusion | flops 393216 | bytes 4719104 | tf_op jit(solution)/shard_map/while/body/eval_jaxpr/cond/branch_1_fun/scatter-add | solution.py:42
  416.1 4.4 fusion.21
  420.6 4.6 scatter_fusion
  425.2 1.4 convert_element_type.48
  426.6 2.7 copy.14
  429.4 1.4 convert_element_type.49
  430.8 2.6 copy.16
  433.4 36.2 %reduce-scatter.7.cloned.1.call-done = bf16[384,256]{1,0:T(8,128)(2,1)} async-done(((bf16[3072,256]{1,0:T(8,128)(2,1)}), bf16[384,256]{1,0:T(8,128)(2,1)}) %reduce-scatter.7.cloned.1.call-update) | async-done | bytes 196624
  469.6 1.7 copy.15
  471.4 40.0 %reduce-scatter.9.cloned.1.call-done = bf16[384,256]{1,0:T(8,128)(2,1)} async-done(((bf16[3072,256]{1,0:T(8,128)(2,1)}), bf16[384,256]{1,0:T(8,128)(2,1)}) %reduce-scatter.9.cloned.1.call-update) | async-done | bytes 196624
  511.4 1.7 copy.17
  (56 shorter events, 5.6 us)
Async XLA Ops:
  7.2 174.2 %all-gather.3.cloned.1.call-start = ((), (), s32[]{:S(2)}) async-start(), calls=%async_computation.3 | async-start | bytes 9732096 | tf_op jit(solution)/shard_map/all_gather | solution.py:60
  9.1 219.5 %all-gather.5.cloned.1.call-start = ((), (), s32[]{:S(2)}) async-start(), calls=%async_computation.4 | async-start | bytes 9732096 | tf_op jit(solution)/shard_map/all_gather | solution.py:61
  16.9 7.9 %copy-start.4 = (s32[512]{0:T(512)S(1)}, s32[512]{0:T(512)}, u32[]{:S(2)}) copy-start(s32[512]{0:T(512)} %param.18) | copy-start | bytes 6148
  16.9 143.7 %all-to-all-start = ((bf16[32,2,768,96]{2,3,1,0:T(8,128)(2,1)}), bf16[32,2,768,96]{2,3,1,0:T(8,128)(2,1)}, u32[]{:S(2)}, u32[]{:S(2)}) async-start(bf16[32,2,768,96]{2,3,1,0:T(8,128)(2,1)} %stack.2), calls=%async_computation | async-start | bytes 18874368 | tf_op jit(solution)/shard_map/all_to_all | solution.py:64
  24.7 444.9 %reduce-scatter.7.cloned.1.call-start = ((), (), s32[]{:S(2)}) async-start(), calls=%async_computation.5 | async-start | bytes 1769472
  181.4 49.6 %copy-start.5 = (s32[4]{0:T(128)S(1)}, s32[4]{0:T(128)}, u32[]{:S(2)}) copy-start(s32[4]{0:T(128)} %param.19) | copy-start | bytes 52
  247.4 3.4 copy-start.2
  250.9 4.1 copy-start.1
  258.1 5.3 %copy-start.3 = (f32[128,768]{1,0:T(8,128)}, f32[128,768]{1,0:T(8,128)S(1)}, u32[]{:S(2)}) copy-start(f32[128,768]{1,0:T(8,128)S(1)} %fusion.6) | copy-start | bytes 1179652 | tf_op jit(solution)/shard_map/while/body/eval_jaxpr/cond
  296.0 3.4 copy-start.2
  299.4 4.1 copy-start.1
  306.6 5.3 %copy-start.3 = (f32[128,768]{1,0:T(8,128)}, f32[128,768]{1,0:T(8,128)S(1)}, u32[]{:S(2)}) copy-start(f32[128,768]{1,0:T(8,128)S(1)} %fusion.6) | copy-start | bytes 1179652 | tf_op jit(solution)/shard_map/while/body/eval_jaxpr/cond
  344.6 3.4 copy-start.2
  348.0 4.1 copy-start.1
  355.2 5.3 %copy-start.3 = (f32[128,768]{1,0:T(8,128)}, f32[128,768]{1,0:T(8,128)S(1)}, u32[]{:S(2)}) copy-start(f32[128,768]{1,0:T(8,128)S(1)} %fusion.6) | copy-start | bytes 1179652 | tf_op jit(solution)/shard_map/while/body/eval_jaxpr/cond
  393.1 3.4 copy-start.2
  396.6 4.1 copy-start.1
  403.8 5.3 %copy-start.3 = (f32[128,768]{1,0:T(8,128)}, f32[128,768]{1,0:T(8,128)S(1)}, u32[]{:S(2)}) copy-start(f32[128,768]{1,0:T(8,128)S(1)} %fusion.6) | copy-start | bytes 1179652 | tf_op jit(solution)/shard_map/while/body/eval_jaxpr/cond
  426.6 2.8 copy-start
  429.4 82.0 %reduce-scatter.9.cloned.1.call-start = ((), (), s32[]{:S(2)}) async-start(), calls=%async_computation.6 | async-start | bytes 1769472
Sparse Core Ops, SparseCore 0:
  10.6 150.3 all-gather.2
  163.6 64.9 all-gather.4
  429.5 40.0 reduce-scatter.6
  472.0 39.3 reduce-scatter.8
